TPU v7x, 32 devices: a whole 2x2x4 slice. The times are simulated.
32 devices in a mesh: wide: 16 (over z, x, core), narrow: 2 (over y).
Axes of the slice: x: 2, y: 2, z: 4, core: 2. Of those that a mesh axis runs over, the one named last changes fastest.
Arguments:
- embeddings: float32 [16384, 512], P(('wide', 'narrow')), may hold values from -2.1 to 2.1
- accum: float32 [16384], P(('wide', 'narrow')), may hold values from 0.01 to 1
- relation: bfloat16 [512, 512], replicated, may hold values from -0.25 to 0.25
- head_index: int32 [2, 16384], P(None, ('wide', 'narrow')), may hold values from 0 to 511
- tail_index: int32 [2, 16384], P(None, ('wide', 'narrow')), may hold values from 0 to 511
- negative_index: int32 [2, 8192], P(None, ('wide', 'narrow')), may hold values from 0 to 511
- partner: int32 [2, 16], replicated, may hold values from 0 to 15, each once within a row
- edge_count: int32 [2, 32], P(None, ('wide', 'narrow')), may hold values from 1 to 512, 8192 in all within a row
Outputs:
- new_embeddings: float32 [16384, 512], P(('wide', 'narrow'))
- new_accum: float32 [16384], P(('wide', 'narrow'))
- relation_grad: float32 [512, 512], replicated
- edge_losses: float32 [2, 16384], P(None, ('wide', 'narrow'))
Inputs may be any that keep to these rules, and one draw needn't show every extreme that they name: Each row of partner is a permutation of the wide indices. `edge_count`: in each bucket step the counts of all devices sum to half of all slots, and some device has exactly 512.
All inputs are finite; a program needn't handle non-finite values.
Results may differ from a plain program's by a relative error of at most 0.0064.
Values may be sent and summed in bfloat16 or wider, within the bound.
A program may use at most 64 MiB of HBM per device.

v0:
```python
import jax
import jax.numpy as jnp
from jax import lax
from jax.sharding import PartitionSpec as P

LEARN_RATE = 0.1
EPSILON = 1e-06


def as_sent(array):

    def short(part):
        return part.astype(jnp.bfloat16) if part.dtype == jnp.float32 else part

    return jax.tree.map(short, array)


def split_rows(values, parts):
    return values.reshape((parts, values.shape[0] // parts) + values.shape[1:])


def join_rows(values):
    return values.reshape((values.shape[0] * values.shape[1],) + values.shape[2:])


def invert(order):
    positions = jnp.arange(order.shape[0], dtype=jnp.int32)
    return jnp.sum(jnp.where(order[:, None] == positions[None, :], positions[:, None], 0), axis=0)


def bucket_terms(query_bf, tail_ids, block_bf, neg_ids):
    tail_rows = jnp.take(block_bf, tail_ids, axis=0)
    own_negs = jnp.take(block_bf, neg_ids, axis=0)
    negatives = lax.all_gather(own_negs, "narrow", axis=0, tiled=True)
    positive = jnp.sum(query_bf.astype(jnp.float32) * tail_rows.astype(jnp.float32), axis=1)
    scores = lax.dot_general(
        query_bf, negatives, (((1,), (1,)), ((), ())), preferred_element_type=jnp.float32
    )
    exp_pos = jnp.exp(positive)
    exp_neg = jnp.exp(scores)
    total = exp_pos + jnp.sum(exp_neg, axis=1)
    losses = jnp.log(total) - positive
    pos_weight = exp_pos / total - 1.0
    weights = (exp_neg / total[:, None]).astype(jnp.bfloat16)
    query_grad = pos_weight[:, None] * tail_rows.astype(jnp.float32) + jnp.dot(
        weights, negatives, preferred_element_type=jnp.float32
    )
    tail_pos = pos_weight[:, None] * query_bf.astype(jnp.float32)
    negative_grad = lax.psum_scatter(
        lax.dot_general(
            weights, query_bf, (((0,), (0,)), ((), ())), preferred_element_type=jnp.float32
        ).astype(jnp.bfloat16),
        "narrow",
        scatter_dimension=0,
        tiled=True,
    ).astype(jnp.float32)
    tail_grad = (
        jnp.zeros(block_bf.shape, jnp.float32)
        .at[tail_ids]
        .add(tail_pos)
        .at[neg_ids]
        .add(negative_grad)
    )
    return (losses, query_grad, tail_grad)


def on_device(
    embeddings, accum, relation, head_index, tail_index, negative_index, partner, edge_count
):
    wide_size = lax.axis_size("wide")
    step_total = head_index.shape[0]
    positions = jnp.arange(head_index.shape[1], dtype=jnp.int32)
    relation_sum = jnp.zeros(relation.shape, jnp.float32)
    loss_rows = []
    for step in range(step_total):
        order = partner[step]
        inverse = invert(order)
        live = positions < edge_count[step, 0]
        block_bf = embeddings.astype(jnp.bfloat16)
        head_rows = jnp.take(block_bf, head_index[step], axis=0)
        query = jnp.dot(head_rows, relation, preferred_element_type=jnp.float32)
        query_bf = jnp.where(live[:, None], query, 0.0).astype(jnp.bfloat16)
        outgoing = lax.all_to_all(
            split_rows(block_bf, wide_size), "wide", split_axis=0, concat_axis=0, tiled=True
        )
        incoming = lax.all_to_all(
            jnp.take(outgoing, order, axis=0), "wide", split_axis=0, concat_axis=0, tiled=True
        )
        losses, query_grad, tail_grad = bucket_terms(
            query_bf, tail_index[step], join_rows(incoming), negative_index[step]
        )
        sent = lax.all_to_all(
            split_rows(tail_grad, wide_size).astype(jnp.bfloat16),
            "wide",
            split_axis=0,
            concat_axis=0,
            tiled=True,
        ).astype(jnp.float32)
        back = lax.all_to_all(
            as_sent(jnp.take(sent, inverse, axis=0)),
            "wide",
            split_axis=0,
            concat_axis=0,
            tiled=True,
        )
        owner_grad = join_rows(back)
        grad_bf = jnp.where(live[:, None], query_grad, 0.0).astype(jnp.bfloat16)
        head_term = lax.dot_general(
            grad_bf, relation, (((1,), (1,)), ((), ())), preferred_element_type=jnp.float32
        )
        head_grad = jnp.zeros(embeddings.shape, jnp.float32).at[head_index[step]].add(head_term)
        relation_part = lax.dot_general(
            head_rows, grad_bf, (((0,), (0,)), ((), ())), preferred_element_type=jnp.float32
        )
        relation_sum = relation_sum + relation_part
        grads = head_grad + owner_grad
        accum = accum + jnp.mean(grads * grads, axis=1)
        embeddings = embeddings - LEARN_RATE * grads / (jnp.sqrt(accum)[:, None] + EPSILON)
        loss_rows.append(jnp.where(live, losses, 0.0))
    relation_sum = lax.psum(relation_sum, ("wide", "narrow"))
    return (embeddings, accum, relation_sum, jnp.stack(loss_rows))


def solution(mesh):
    in_specs = (
        P(("wide", "narrow"), None),
        P(("wide", "narrow")),
        P(),
        P(None, ("wide", "narrow")),
        P(None, ("wide", "narrow")),
        P(None, ("wide", "narrow")),
        P(),
        P(None, ("wide", "narrow")),
    )
    out_specs = (
        P(("wide", "narrow"), None),
        P(("wide", "narrow")),
        P(),
        P(None, ("wide", "narrow")),
    )
    return jax.shard_map(
        on_device, mesh=mesh, in_specs=in_specs, out_specs=out_specs, check_vma=False
    )
```

profile of v0, /device:TPU:0, one launch (start us, length us, event | category | flops | bytes accessed | tf_op | source)
XLA Modules:
  0.0 378.0 jit_solution(17429168418496107216)
XLA Ops:
  7.2 2.1 convert_element_type.88
  9.3 7.5 %all-to-all-start = ((bf16[16,32,512]{2,1,0:T(8,128)(2,1)}), bf16[16,32,512]{2,1,0:T(8,128)(2,1)S(1)}, u32[]{:S(2)}, u32[]{:S(2)}) async-start(bf16[16,32,512]{2,1,0:T(8,128)(2,1)} %bitcast.6), calls=%async_computation | async-start | bytes 1048576 | tf_op jit(solution)/shard_map/all_to_all | solution.py:83
  16.9 3.1 gather_fusion
  21.4 9.7 %all-to-all-done = bf16[16,32,512]{2,1,0:T(8,128)(2,1)S(1)} async-done(((bf16[16,32,512]{2,1,0:T(8,128)(2,1)}), bf16[16,32,512]{2,1,0:T(8,128)(2,1)S(1)}, u32[]{:S(2)}, u32[]{:S(2)}) %all-to-all-start) | async-done | bytes 524320 | tf_op jit(solution)/shard_map/all_to_all | solution.py:83
  32.6 4.2 %all-to-all-start.1 = ((bf16[16,32,512]{2,1,0:T(8,128)(2,1)}), bf16[16,32,512]{2,1,0:T(8,128)(2,1)S(1)}, u32[]{:S(2)}, u32[]{:S(2)}) async-start(bf16[16,32,512]{2,1,0:T(8,128)(2,1)} %broadcast_select_fusion.2), calls=%async_computation.1 | async-start | bytes 1048576 | tf_op jit(solution)/shard_map/all_to_all | solution.py:86
  38.8 12.3 %all-to-all-done.1 = bf16[16,32,512]{2,1,0:T(8,128)(2,1)S(1)} async-done(((bf16[16,32,512]{2,1,0:T(8,128)(2,1)}), bf16[16,32,512]{2,1,0:T(8,128)(2,1)S(1)}, u32[]{:S(2)}, u32[]{:S(2)}) %all-to-all-start.1) | async-done | bytes 524320 | tf_op jit(solution)/shard_map/all_to_all | solution.py:86
  54.5 9.0 %all_gather.6 = bf16[512,512]{1,0:T(8,128)(2,1)S(1)} all-gather(bf16[256,512]{1,0:T(8,128)(2,1)S(1)} %broadcast_select_fusion.7), channel_id=1, replica_groups=mesh['wide'=16,'narrow'=2] {'narrow'}, dimensions={0}, use_global_device_ids=true | all-gather | bytes 786432 | tf_op jit(solution)/shard_map/all_gather | solution.py:34
  68.4 4.5 %scatter_custom_fusion = f32[512,512]{1,0:T(8,128)S(1)} fusion(s32[512]{0:T(512)S(1)} %bitcast.92, f32[512,512]{1,0:T(8,128)} %copy.30, f32[]{:T(128)} %constant.39.clone.1), kind=kCustom, calls=%fused_computation.49 | custom fusion | flops 262144 | bytes 1049088 | tf_op jit(solution)/shard_map/scatter-add | solution.py:60
  72.9 8.6 %reduce-scatter.3.cloned.1.call-done = bf16[256,512]{1,0:T(8,128)(2,1)} async-done(((bf16[512,512]{1,0:T(8,128)(2,1)}), bf16[256,512]{1,0:T(8,128)(2,1)}) %reduce-scatter.3.cloned.1.call-update) | async-done | bytes 262160 | tf_op jit(solution)/shard_map/reduce_scatter | solution.py:49
  81.5 2.9 scatter_custom_fusion.1
  85.2 5.6 %all-to-all-start.2 = ((bf16[16,32,512]{2,1,0:T(8,128)(2,1)}), bf16[16,32,512]{2,1,0:T(8,128)(2,1)S(1)}, u32[]{:S(2)}, u32[]{:S(2)}) async-start(bf16[16,32,512]{2,1,0:T(8,128)(2,1)} %bitcast.11), calls=%async_computation.3 | async-start | bytes 1048576 | tf_op jit(solution)/shard_map/all_to_all | solution.py:92
  91.0 14.1 %all-to-all-done.2 = bf16[16,32,512]{2,1,0:T(8,128)(2,1)S(1)} async-done(((bf16[16,32,512]{2,1,0:T(8,128)(2,1)}), bf16[16,32,512]{2,1,0:T(8,128)(2,1)S(1)}, u32[]{:S(2)}, u32[]{:S(2)}) %all-to-all-start.2) | async-done | bytes 524320 | tf_op jit(solution)/shard_map/all_to_all | solution.py:92
  106.7 4.4 %all-to-all-start.3 = ((bf16[16,32,512]{2,1,0:T(8,128)(2,1)}), bf16[16,32,512]{2,1,0:T(8,128)(2,1)}, u32[]{:S(2)}, u32[]{:S(2)}) async-start(bf16[16,32,512]{2,1,0:T(8,128)(2,1)} %select_convert_fusion.1), calls=%async_computation.4 | async-start | bytes 1048576 | tf_op jit(solution)/shard_map/all_to_all | solution.py:99
  113.4 11.9 %all-to-all-done.3 = bf16[16,32,512]{2,1,0:T(8,128)(2,1)} async-done(((bf16[16,32,512]{2,1,0:T(8,128)(2,1)}), bf16[16,32,512]{2,1,0:T(8,128)(2,1)}, u32[]{:S(2)}, u32[]{:S(2)}) %all-to-all-start.3) | async-done | bytes 524320 | tf_op jit(solution)/shard_map/all_to_all | solution.py:99
  126.5 4.2 %scatter_fusion = f32[512,512]{1,0:T(8,128)S(1)} fusion(f32[512,512]{1,0:T(8,128)S(1)} %bitcast_convert_fusion.1, s32[512]{0:T(512)S(1)} %bitcast.84, f32[512,512]{1,0:T(8,128)S(1)} %fusion.28), kind=kCustom, calls=%fused_computation.12 | custom fusion | flops 262144 | bytes 3147776 | tf_op jit(solution)/shard_map/scatter-add | solution.py:111
  133.0 4.2 %all-to-all-start.4 = ((bf16[16,32,512]{2,1,0:T(8,128)(2,1)}), bf16[16,32,512]{2,1,0:T(8,128)(2,1)S(1)}, u32[]{:S(2)}, u32[]{:S(2)}) async-start(bf16[16,32,512]{2,1,0:T(8,128)(2,1)} %bitcast.21), calls=%async_computation.5 | async-start | bytes 1048576 | tf_op jit(solution)/shard_map/all_to_all | solution.py:83
  137.2 14.2 %all-to-all-done.4 = bf16[16,32,512]{2,1,0:T(8,128)(2,1)S(1)} async-done(((bf16[16,32,512]{2,1,0:T(8,128)(2,1)}), bf16[16,32,512]{2,1,0:T(8,128)(2,1)S(1)}, u32[]{:S(2)}, u32[]{:S(2)}) %all-to-all-start.4) | async-done | bytes 524320 | tf_op jit(solution)/shard_map/all_to_all | solution.py:83
  152.9 4.2 %all-to-all-start.5 = ((bf16[16,32,512]{2,1,0:T(8,128)(2,1)}), bf16[16,32,512]{2,1,0:T(8,128)(2,1)S(1)}, u32[]{:S(2)}, u32[]{:S(2)}) async-start(bf16[16,32,512]{2,1,0:T(8,128)(2,1)} %broadcast_select_fusion), calls=%async_computation.6 | async-start | bytes 1048576 | tf_op jit(solution)/shard_map/all_to_all | solution.py:86
  157.9 3.8 gather_fusion.5
  161.6 9.7 %all-to-all-done.5 = bf16[16,32,512]{2,1,0:T(8,128)(2,1)S(1)} async-done(((bf16[16,32,512]{2,1,0:T(8,128)(2,1)}), bf16[16,32,512]{2,1,0:T(8,128)(2,1)S(1)}, u32[]{:S(2)}, u32[]{:S(2)}) %all-to-all-start.5) | async-done | bytes 524320 | tf_op jit(solution)/shard_map/all_to_all | solution.py:86
  172.5 2.0 gather_fusion.7
  174.9 9.2 %all_gather.7 = bf16[512,512]{1,0:T(8,128)(2,1)S(1)} all-gather(bf16[256,512]{1,0:T(8,128)(2,1)S(1)} %broadcast_select_fusion.6), channel_id=1, replica_groups=mesh['wide'=16,'narrow'=2] {'narrow'}, dimensions={0}, use_global_device_ids=true | all-gather | bytes 786432 | tf_op jit(solution)/shard_map/all_gather | solution.py:34
  190.2 4.5 %scatter_custom_fusion.3 = f32[512,512]{1,0:T(8,128)S(1)} fusion(s32[512]{0:T(512)S(1)} %bitcast.91, f32[512,512]{1,0:T(8,128)} %copy.34, f32[]{:T(128)} %constant.39.clone.1), kind=kCustom, calls=%fused_computation.47 | custom fusion | flops 262144 | bytes 1049088 | tf_op jit(solution)/shard_map/scatter-add | solution.py:60
  194.7 6.5 %reduce-scatter.5.cloned.1.call-done = bf16[256,512]{1,0:T(8,128)(2,1)} async-done(((bf16[512,512]{1,0:T(8,128)(2,1)}), bf16[256,512]{1,0:T(8,128)(2,1)}) %reduce-scatter.5.cloned.1.call-update) | async-done | bytes 262160 | tf_op jit(solution)/shard_map/reduce_scatter | solution.py:49
  201.2 3.1 scatter_custom_fusion.4
  205.2 5.7 %all-to-all-start.6 = ((bf16[16,32,512]{2,1,0:T(8,128)(2,1)}), bf16[16,32,512]{2,1,0:T(8,128)(2,1)}, u32[]{:S(2)}, u32[]{:S(2)}) async-start(bf16[16,32,512]{2,1,0:T(8,128)(2,1)} %bitcast.72), calls=%async_computation.8 | async-start | bytes 1048576 | tf_op jit(solution)/shard_map/all_to_all | solution.py:92
  213.3 11.9 %all-to-all-done.6 = bf16[16,32,512]{2,1,0:T(8,128)(2,1)} async-done(((bf16[16,32,512]{2,1,0:T(8,128)(2,1)}), bf16[16,32,512]{2,1,0:T(8,128)(2,1)}, u32[]{:S(2)}, u32[]{:S(2)}) %all-to-all-start.6) | async-done | bytes 524320 | tf_op jit(solution)/shard_map/all_to_all | solution.py:92
  227.8 4.4 %all-to-all-start.7 = ((bf16[16,32,512]{2,1,0:T(8,128)(2,1)}), bf16[16,32,512]{2,1,0:T(8,128)(2,1)}, u32[]{:S(2)}, u32[]{:S(2)}) async-start(bf16[16,32,512]{2,1,0:T(8,128)(2,1)} %select_convert_fusion), calls=%async_computation.9 | async-start | bytes 1048576 | tf_op jit(solution)/shard_map/all_to_all | solution.py:99
  239.4 7.1 %all-to-all-done.7 = bf16[16,32,512]{2,1,0:T(8,128)(2,1)} async-done(((bf16[16,32,512]{2,1,0:T(8,128)(2,1)}), bf16[16,32,512]{2,1,0:T(8,128)(2,1)}, u32[]{:S(2)}, u32[]{:S(2)}) %all-to-all-start.7) | async-done | bytes 524320 | tf_op jit(solution)/shard_map/all_to_all | solution.py:99
  247.7 4.7 %scatter_fusion.1 = f32[512,512]{1,0:T(8,128)S(1)} fusion(f32[512,512]{1,0:T(8,128)S(1)} %bitcast_convert_fusion, s32[512]{0:T(512)S(1)} %bitcast.83, f32[512,512]{1,0:T(8,128)} %fusion.29), kind=kCustom, calls=%fused_computation.15 | custom fusion | flops 262144 | bytes 3147776 | tf_op jit(solution)/shard_map/scatter-add | solution.py:111
  255.0 114.2 %all-reduce.2.cloned.1.call-done = f32[512,512]{1,0:T(8,128)} async-done(((f32[512,512]{1,0:T(8,128)}), f32[512,512]{1,0:T(8,128)}) %all-reduce.2.cloned.1.call-update) | async-done | bytes 1048592 | tf_op jit(solution)/shard_map/psum | solution.py:120
  369.2 2.3 copy.49
  (133 shorter events, 47.9 us)
Async XLA Ops:
  7.2 56.4 %copy-start = (bf16[512,512]{1,0:T(8,128)(2,1)S(1)}, bf16[512,512]{1,0:T(8,128)(2,1)}, u32[]{:S(2)}) copy-start(bf16[512,512]{1,0:T(8,128)(2,1)} %param.18) | copy-start | bytes 1572868
  9.3 7.5 %copy-start.20 = (s32[2,16]{1,0:T(2,128)S(1)}, s32[2,16]{1,0:T(2,128)}, u32[]{:S(2)}) copy-start(s32[2,16]{1,0:T(2,128)} %param.22) | copy-start | bytes 388
  9.3 7.6 %copy-start.17 = (s32[2,512]{1,0:T(2,128)S(1)}, s32[2,512]{1,0:T(2,128)}, u32[]{:S(2)}) copy-start(s32[2,512]{1,0:T(2,128)} %param.19) | copy-start | bytes 12292
  9.3 21.8 %all-to-all-start = ((bf16[16,32,512]{2,1,0:T(8,128)(2,1)}), bf16[16,32,512]{2,1,0:T(8,128)(2,1)S(1)}, u32[]{:S(2)}, u32[]{:S(2)}) async-start(bf16[16,32,512]{2,1,0:T(8,128)(2,1)} %bitcast.6), calls=%async_computation | async-start | bytes 1048576 | tf_op jit(solution)/shard_map/all_to_all | solution.py:83
  20.0 0.7 copy-start.19
  20.7 0.7 copy-start.16
  32.6 18.4 %all-to-all-start.1 = ((bf16[16,32,512]{2,1,0:T(8,128)(2,1)}), bf16[16,32,512]{2,1,0:T(8,128)(2,1)S(1)}, u32[]{:S(2)}, u32[]{:S(2)}) async-start(bf16[16,32,512]{2,1,0:T(8,128)(2,1)} %broadcast_select_fusion.2), calls=%async_computation.1 | async-start | bytes 1048576 | tf_op jit(solution)/shard_map/all_to_all | solution.py:86
  36.8 44.7 %reduce-scatter.3.cloned.1.call-start = ((), (), s32[]{:S(2)}) async-start(), calls=%async_computation.10 | async-start | bytes 786432 | tf_op jit(solution)/shard_map/reduce_scatter | solution.py:49
  54.4 9.1 %copy-start.15 = (bf16[512,512]{0,1:T(8,128)(2,1)}, bf16[512,512]{0,1:T(8,128)(2,1)S(1)}, u32[]{:S(2)}) copy-start(bf16[512,512]{0,1:T(8,128)(2,1)S(1)} %copy.28) | copy-start | bytes 1572868
  64.6 1.0 copy-start.12
  85.2 19.9 %all-to-all-start.2 = ((bf16[16,32,512]{2,1,0:T(8,128)(2,1)}), bf16[16,32,512]{2,1,0:T(8,128)(2,1)S(1)}, u32[]{:S(2)}, u32[]{:S(2)}) async-start(bf16[16,32,512]{2,1,0:T(8,128)(2,1)} %bitcast.11), calls=%async_computation.3 | async-start | bytes 1048576 | tf_op jit(solution)/shard_map/all_to_all | solution.py:92
  106.7 4.4 %copy-start.13 = (f32[512,512]{0,1:T(8,128)S(1)}, f32[512,512]{0,1:T(8,128)}, u32[]{:S(2)}) copy-start(f32[512,512]{0,1:T(8,128)} %copy-done.12) | copy-start | bytes 3145732
  106.7 18.7 %all-to-all-start.3 = ((bf16[16,32,512]{2,1,0:T(8,128)(2,1)}), bf16[16,32,512]{2,1,0:T(8,128)(2,1)}, u32[]{:S(2)}, u32[]{:S(2)}) async-start(bf16[16,32,512]{2,1,0:T(8,128)(2,1)} %select_convert_fusion.1), calls=%async_computation.4 | async-start | bytes 1048576 | tf_op jit(solution)/shard_map/all_to_all | solution.py:99
  112.6 0.8 copy-start.6
  130.7 0.7 copy-start.18
  130.7 1.2 copy-start.1
  133.0 18.4 %all-to-all-start.4 = ((bf16[16,32,512]{2,1,0:T(8,128)(2,1)}), bf16[16,32,512]{2,1,0:T(8,128)(2,1)S(1)}, u32[]{:S(2)}, u32[]{:S(2)}) async-start(bf16[16,32,512]{2,1,0:T(8,128)(2,1)} %bitcast.21), calls=%async_computation.5 | async-start | bytes 1048576 | tf_op jit(solution)/shard_map/all_to_all | solution.py:83
  152.9 18.4 %all-to-all-start.5 = ((bf16[16,32,512]{2,1,0:T(8,128)(2,1)}), bf16[16,32,512]{2,1,0:T(8,128)(2,1)S(1)}, u32[]{:S(2)}, u32[]{:S(2)}) async-start(bf16[16,32,512]{2,1,0:T(8,128)(2,1)} %broadcast_select_fusion), calls=%async_computation.6 | async-start | bytes 1048576 | tf_op jit(solution)/shard_map/all_to_all | solution.py:86
  157.1 44.1 %reduce-scatter.5.cloned.1.call-start = ((), (), s32[]{:S(2)}) async-start(), calls=%async_computation.11 | async-start | bytes 786432 | tf_op jit(solution)/shard_map/reduce_scatter | solution.py:49
  174.7 9.3 %copy-start.14 = (bf16[512,512]{0,1:T(8,128)(2,1)}, bf16[512,512]{0,1:T(8,128)(2,1)S(1)}, u32[]{:S(2)}) copy-start(bf16[512,512]{0,1:T(8,128)(2,1)S(1)} %copy.32) | copy-start | bytes 1572868
  174.8 9.2 %copy-start.7 = (bf16[512,512]{1,0:T(8,128)(2,1)S(1)}, bf16[512,512]{1,0:T(8,128)(2,1)}, u32[]{:S(2)}) copy-start(bf16[512,512]{1,0:T(8,128)(2,1)} %gather_fusion.5) | copy-start | bytes 1572868
  184.0 0.8 copy-start.3
  184.6 0.8 copy-start.5
  185.3 1.0 copy-start.11
  205.2 20.0 %all-to-all-start.6 = ((bf16[16,32,512]{2,1,0:T(8,128)(2,1)}), bf16[16,32,512]{2,1,0:T(8,128)(2,1)}, u32[]{:S(2)}, u32[]{:S(2)}) async-start(bf16[16,32,512]{2,1,0:T(8,128)(2,1)} %bitcast.72), calls=%async_computation.8 | async-start | bytes 1048576 | tf_op jit(solution)/shard_map/all_to_all | solution.py:92
  227.8 4.4 %copy-start.4 = (bf16[512,512]{1,0:T(8,128)(2,1)S(1)}, bf16[512,512]{1,0:T(8,128)(2,1)}, u32[]{:S(2)}) copy-start(bf16[512,512]{1,0:T(8,128)(2,1)} %copy-done.3) | copy-start | bytes 1572868
  227.8 18.8 %all-to-all-start.7 = ((bf16[16,32,512]{2,1,0:T(8,128)(2,1)}), bf16[16,32,512]{2,1,0:T(8,128)(2,1)}, u32[]{:S(2)}, u32[]{:S(2)}) async-start(bf16[16,32,512]{2,1,0:T(8,128)(2,1)} %select_convert_fusion), calls=%async_computation.9 | async-start | bytes 1048576 | tf_op jit(solution)/shard_map/all_to_all | solution.py:99
  232.2 137.1 %all-reduce.2.cloned.1.call-start = ((), (), s32[]{:S(2)}) async-start(), calls=%async_computation.12 | async-start | bytes 2097152 | tf_op jit(solution)/shard_map/psum | solution.py:120
  232.2 2.7 copy-start.8
  234.2 0.8 copy-start.9
  236.6 1.4 copy-start.10
  252.4 1.2 copy-start.2
  (1 other events, 0.7 us)
Sparse Core Ops, SparseCore 0:
  67.0 14.3 reduce-scatter.2
  187.7 13.4 reduce-scatter.4
  238.2 131.0 all-reduce.1
where the time goes:
time: 380 us; the launch traced here: 378 us
  waiting for transfers between devices  220 us (58%)
  other arithmetic  42.3 us (11%)
  starting transfers between devices  40.2 us (11%)
  local copies, waits for them, and re-layouts  29.1 us (8%)
  blocking collectives  18.2 us (5%)
  between operations  14.4 us (4%)
  matrix products  13.4 us (4%)
    psum x1, waiting for transfers between devices, on_device(): relation_sum = lax.psum(relation_sum, ('wide', 'narrow'))  114 us
    all_to_all x2, waiting for transfers between devices, on_device(): lax.all_to_all(split_rows(tail_grad, wide_size).astype(jnp.bfloat16), 'wi...  26.1 us
    all_to_all x2, waiting for transfers between devices, on_device(): lax.all_to_all(split_rows(block_bf, wide_size), 'wide', split_axis=0, con...  23.9 us
    all_to_all x2, waiting for transfers between devices, on_device(): lax.all_to_all(jnp.take(outgoing, order, axis=0), 'wide', split_axis=0, c...  22 us
    all_to_all x2, waiting for transfers between devices, on_device(): lax.all_to_all(as_sent(jnp.take(sent, inverse, axis=0)), 'wide', split_ax...  19.1 us
    all_gather x2, blocking collectives, bucket_terms(): negatives = lax.all_gather(own_negs, 'narrow', axis=0, tiled=True)  18.2 us
    scatter-add x4, other arithmetic, bucket_terms(): tail_grad = jnp.zeros(block_bf.shape, jnp.float32).at[tail_ids].add(tail_...  15.1 us
    reduce_scatter x2, waiting for transfers between devices, bucket_terms(): lax.psum_scatter(lax.dot_general(weights, query_bf, (((0,), (0,)), ((), (...  15.1 us
  transfers between devices with their start and end apart: 11, of which 11 were waited for; matrix products, arithmetic and copies ran while one was open for 11% of the time, Pallas kernels for 0%

commit v1 on v0

--- a/solution.py
+++ b/solution.py
@@ -117,7 +117,8 @@
         accum = accum + jnp.mean(grads * grads, axis=1)
         embeddings = embeddings - LEARN_RATE * grads / (jnp.sqrt(accum)[:, None] + EPSILON)
         loss_rows.append(jnp.where(live, losses, 0.0))
-    relation_sum = lax.psum(relation_sum, ("wide", "narrow"))
+    shards = lax.all_gather(relation_sum, ("wide", "narrow"))
+    relation_sum = jnp.sum(shards, axis=0)
     return (embeddings, accum, relation_sum, jnp.stack(loss_rows))
 
 

time: 380 us -> 435 us (1.14)
  waiting for transfers between devices: 220 us -> 250 us
  other arithmetic: 42.3 us -> 59.4 us
  starting transfers between devices: 40.2 us -> 46.2 us
  matrix products: 13.4 us -> 19.3 us
    all_gather x0 -> x1, waiting for transfers between devices: none -> 144 us  [on_device(): shards = lax.all_gather(relation_sum, ('wide', 'narrow'))]
    psum x1 -> x0, waiting for transfers between devices: 114 us -> none  [on_device(): relation_sum = lax.psum(relation_sum, ('wide', 'narrow'))]
    reduce_sum x0 -> x1, other arithmetic: none -> 13.2 us  [on_device(): relation_sum = jnp.sum(shards, axis=0)]
    reduce_scatter x2, waiting for transfers between devices: 15.1 us -> 6.01 us  [bucket_terms(): lax.psum_scatter(lax.dot_general(weights, query_bf, (((0,), (0,)), ((), (...]
    all_to_all x2, waiting for transfers between devices: 26.1 us -> 34.4 us  [on_device(): lax.all_to_all(split_rows(tail_grad, wide_size).astype(jnp.bfloat16), 'wi...]
    all_to_all x2, starting transfers between devices: 8.76 us -> 15.5 us  [on_device(): lax.all_to_all(as_sent(jnp.take(sent, inverse, axis=0)), 'wide', split_ax...]
    unnamed x45 -> x24, local copies, waits for them, and re-layouts: 9.04 us -> 2.75 us
  transfers between devices with their start and end apart: 11 -> 11, of which waited for: 11 -> 10; matrix products, arithmetic and copies ran while one was open for 11% -> 13% of each run, Pallas kernels for 0% -> 0%
where the time goes in v1:
time: 435 us; the launch traced here: 433 us
  waiting for transfers between devices  250 us (57%)
  other arithmetic  59.4 us (14%)
  starting transfers between devices  46.2 us (11%)
  local copies, waits for them, and re-layouts  26.5 us (6%)
  matrix products  19.3 us (4%)
  blocking collectives  18 us (4%)
  between operations  14.3 us (3%)
    all_gather x1, waiting for transfers between devices, on_device(): shards = lax.all_gather(relation_sum, ('wide', 'narrow'))  144 us
    all_to_all x2, waiting for transfers between devices, on_device(): lax.all_to_all(split_rows(tail_grad, wide_size).astype(jnp.bfloat16), 'wi...  34.4 us
    all_to_all x2, waiting for transfers between devices, on_device(): lax.all_to_all(split_rows(block_bf, wide_size), 'wide', split_axis=0, con...  22.2 us
    all_to_all x2, waiting for transfers between devices, on_device(): lax.all_to_all(jnp.take(outgoing, order, axis=0), 'wide', split_axis=0, c...  21.9 us
    all_to_all x2, waiting for transfers between devices, on_device(): lax.all_to_all(as_sent(jnp.take(sent, inverse, axis=0)), 'wide', split_ax...  20.6 us
    all_gather x2, blocking collectives, bucket_terms(): negatives = lax.all_gather(own_negs, 'narrow', axis=0, tiled=True)  18 us
    all_to_all x2, starting transfers between devices, on_device(): lax.all_to_all(as_sent(jnp.take(sent, inverse, axis=0)), 'wide', split_ax...  15.5 us
    scatter-add x4, other arithmetic, bucket_terms(): tail_grad = jnp.zeros(block_bf.shape, jnp.float32).at[tail_ids].add(tail_...  14.9 us
  transfers between devices with their start and end apart: 11, of which 10 were waited for; matrix products, arithmetic and copies ran while one was open for 13% of the time, Pallas kernels for 0%

profile of v1, /device:TPU:0, one launch (start us, length us, event | category | flops | bytes accessed | tf_op | source)
XLA Modules:
  0.0 433.3 jit_solution(2818424136673507374)
XLA Ops:
  9.3 7.4 %all-to-all-start = ((bf16[16,32,512]{2,1,0:T(8,128)(2,1)}), bf16[16,32,512]{2,1,0:T(8,128)(2,1)S(1)}, u32[]{:S(2)}, u32[]{:S(2)}) async-start(bf16[16,32,512]{2,1,0:T(8,128)(2,1)} %bitcast.6), calls=%async_computation | async-start | bytes 1048576 | tf_op jit(solution)/shard_map/all_to_all | solution.py:83
  18.3 3.2 gather_fusion
  23.0 8.0 %all-to-all-done = bf16[16,32,512]{2,1,0:T(8,128)(2,1)S(1)} async-done(((bf16[16,32,512]{2,1,0:T(8,128)(2,1)}), bf16[16,32,512]{2,1,0:T(8,128)(2,1)S(1)}, u32[]{:S(2)}, u32[]{:S(2)}) %all-to-all-start) | async-done | bytes 524320 | tf_op jit(solution)/shard_map/all_to_all | solution.py:83
  32.5 4.2 all-to-all-start.1
  38.7 12.2 %all-to-all-done.1 = bf16[16,32,512]{2,1,0:T(8,128)(2,1)S(1)} async-done(((bf16[16,32,512]{2,1,0:T(8,128)(2,1)}), bf16[16,32,512]{2,1,0:T(8,128)(2,1)S(1)}, u32[]{:S(2)}, u32[]{:S(2)}) %all-to-all-start.1) | async-done | bytes 524320 | tf_op jit(solution)/shard_map/all_to_all | solution.py:86
  55.2 9.0 %all_gather.12 = bf16[512,512]{1,0:T(8,128)(2,1)S(1)} all-gather(bf16[256,512]{1,0:T(8,128)(2,1)S(1)} %broadcast_select_fusion.7), channel_id=1, replica_groups=mesh['wide'=16,'narrow'=2] {'narrow'}, dimensions={0}, use_global_device_ids=true | all-gather | bytes 786432 | tf_op jit(solution)/shard_map/all_gather | solution.py:34
  72.9 4.5 %scatter_custom_fusion = f32[512,512]{1,0:T(8,128)S(1)} fusion(s32[512]{0:T(512)S(1)} %bitcast.94, f32[512,512]{1,0:T(8,128)} %copy.30, f32[]{:T(128)} %constant.39.clone.1), kind=kCustom, calls=%fused_computation.49 | custom fusion | flops 262144 | bytes 1049088 | tf_op jit(solution)/shard_map/scatter-add | solution.py:60
  77.4 6.0 %reduce-scatter.3.cloned.1.call-done = bf16[256,512]{1,0:T(8,128)(2,1)} async-done(((bf16[512,512]{1,0:T(8,128)(2,1)}), bf16[256,512]{1,0:T(8,128)(2,1)}) %reduce-scatter.3.cloned.1.call-update) | async-done | bytes 262160 | tf_op jit(solution)/shard_map/reduce_scatter | solution.py:49
  83.4 2.9 scatter_custom_fusion.1
  87.2 5.6 %all-to-all-start.2 = ((bf16[16,32,512]{2,1,0:T(8,128)(2,1)}), bf16[16,32,512]{2,1,0:T(8,128)(2,1)S(1)}, u32[]{:S(2)}, u32[]{:S(2)}) async-start(bf16[16,32,512]{2,1,0:T(8,128)(2,1)} %bitcast.74), calls=%async_computation.3 | async-start | bytes 1048576 | tf_op jit(solution)/shard_map/all_to_all | solution.py:92
  92.9 14.1 %all-to-all-done.2 = bf16[16,32,512]{2,1,0:T(8,128)(2,1)S(1)} async-done(((bf16[16,32,512]{2,1,0:T(8,128)(2,1)}), bf16[16,32,512]{2,1,0:T(8,128)(2,1)S(1)}, u32[]{:S(2)}, u32[]{:S(2)}) %all-to-all-start.2) | async-done | bytes 524320 | tf_op jit(solution)/shard_map/all_to_all | solution.py:92
  108.6 4.2 all-to-all-start.3
  116.4 10.8 %all-to-all-done.3 = bf16[16,32,512]{2,1,0:T(8,128)(2,1)} async-done(((bf16[16,32,512]{2,1,0:T(8,128)(2,1)}), bf16[16,32,512]{2,1,0:T(8,128)(2,1)}, u32[]{:S(2)}, u32[]{:S(2)}) %all-to-all-start.3) | async-done | bytes 524320 | tf_op jit(solution)/shard_map/all_to_all | solution.py:99
  128.3 4.8 %scatter_fusion = f32[512,512]{1,0:T(8,128)S(1)} fusion(f32[512,512]{1,0:T(8,128)S(1)} %bitcast_convert_fusion.1, s32[512]{0:T(512)S(1)} %bitcast.86, f32[512,512]{1,0:T(8,128)} %fusion.28), kind=kCustom, calls=%fused_computation.12 | custom fusion | flops 262144 | bytes 3147776 | tf_op jit(solution)/shard_map/scatter-add | solution.py:111
  134.4 4.2 all-to-all-start.4
  138.6 14.2 %all-to-all-done.4 = bf16[16,32,512]{2,1,0:T(8,128)(2,1)S(1)} async-done(((bf16[16,32,512]{2,1,0:T(8,128)(2,1)}), bf16[16,32,512]{2,1,0:T(8,128)(2,1)S(1)}, u32[]{:S(2)}, u32[]{:S(2)}) %all-to-all-start.4) | async-done | bytes 524320 | tf_op jit(solution)/shard_map/all_to_all | solution.py:83
  154.3 4.2 all-to-all-start.5
  159.2 3.8 gather_fusion.5
  163.0 9.7 %all-to-all-done.5 = bf16[16,32,512]{2,1,0:T(8,128)(2,1)S(1)} async-done(((bf16[16,32,512]{2,1,0:T(8,128)(2,1)}), bf16[16,32,512]{2,1,0:T(8,128)(2,1)S(1)}, u32[]{:S(2)}, u32[]{:S(2)}) %all-to-all-start.5) | async-done | bytes 524320 | tf_op jit(solution)/shard_map/all_to_all | solution.py:86
  177.0 9.0 %all_gather.13 = bf16[512,512]{1,0:T(8,128)(2,1)S(1)} all-gather(bf16[256,512]{1,0:T(8,128)(2,1)S(1)} %broadcast_select_fusion.6), channel_id=1, replica_groups=mesh['wide'=16,'narrow'=2] {'narrow'}, dimensions={0}, use_global_device_ids=true | all-gather | bytes 786432 | tf_op jit(solution)/shard_map/all_gather | solution.py:34
  195.2 2.7 convolution_add_fusion
  200.4 4.5 %scatter_custom_fusion.3 = f32[512,512]{1,0:T(8,128)S(1)} fusion(s32[512]{0:T(512)S(1)} %bitcast.93, f32[512,512]{1,0:T(8,128)} %copy.34, f32[]{:T(128)} %constant.39.clone.1), kind=kCustom, calls=%fused_computation.47 | custom fusion | flops 262144 | bytes 1049088 | tf_op jit(solution)/shard_map/scatter-add | solution.py:60
  204.9 2.9 scatter_custom_fusion.4
  208.7 4.8 %all-to-all-start.6 = ((bf16[16,32,512]{2,1,0:T(8,128)(2,1)}), bf16[16,32,512]{2,1,0:T(8,128)(2,1)S(1)}, u32[]{:S(2)}, u32[]{:S(2)}) async-start(bf16[16,32,512]{2,1,0:T(8,128)(2,1)} %bitcast.26), calls=%async_computation.8 | async-start | bytes 1048576 | tf_op jit(solution)/shard_map/all_to_all | solution.py:92
  213.7 20.3 %all-to-all-done.6 = bf16[16,32,512]{2,1,0:T(8,128)(2,1)S(1)} async-done(((bf16[16,32,512]{2,1,0:T(8,128)(2,1)}), bf16[16,32,512]{2,1,0:T(8,128)(2,1)S(1)}, u32[]{:S(2)}, u32[]{:S(2)}) %all-to-all-start.6) | async-done | bytes 524320 | tf_op jit(solution)/shard_map/all_to_all | solution.py:92
  235.5 11.3 %all-to-all-start.7 = ((bf16[16,32,512]{2,1,0:T(8,128)(2,1)}), bf16[16,32,512]{2,1,0:T(8,128)(2,1)S(1)}, u32[]{:S(2)}, u32[]{:S(2)}) async-start(bf16[16,32,512]{2,1,0:T(8,128)(2,1)} %select_convert_fusion), calls=%async_computation.9 | async-start | bytes 1048576 | tf_op jit(solution)/shard_map/all_to_all | solution.py:99
  248.8 2.5 fusion.29
  251.3 9.8 %all-to-all-done.7 = bf16[16,32,512]{2,1,0:T(8,128)(2,1)S(1)} async-done(((bf16[16,32,512]{2,1,0:T(8,128)(2,1)}), bf16[16,32,512]{2,1,0:T(8,128)(2,1)S(1)}, u32[]{:S(2)}, u32[]{:S(2)}) %all-to-all-start.7) | async-done | bytes 524320 | tf_op jit(solution)/shard_map/all_to_all | solution.py:99
  261.3 4.7 %scatter_fusion.1 = f32[512,512]{1,0:T(8,128)S(1)} fusion(f32[512,512]{1,0:T(8,128)S(1)} %bitcast_convert_fusion, s32[512]{0:T(512)S(1)} %bitcast.85, f32[512,512]{1,0:T(8,128)} %fusion.29), kind=kCustom, calls=%fused_computation.15 | custom fusion | flops 262144 | bytes 3147776 | tf_op jit(solution)/shard_map/scatter-add | solution.py:111
  266.7 2.6 divide_subtract_fusion
  269.3 144.3 %all-gather.3.cloned.1.call-done = f32[16384,512]{1,0:T(8,128)} async-done(((f32[512,512]{1,0:T(8,128)}), f32[16384,512]{1,0:T(8,128)}) %all-gather.3.cloned.1.call-update) | async-done | bytes 33554448 | tf_op jit(solution)/shard_map/all_gather | solution.py:120
  413.6 13.2 %reduce_sum.97 = f32[512,512]{1,0:T(8,128)} reduce(f32[32,512,512]{2,1,0:T(8,128)} %bitcast.73, f32[]{:T(128)} %constant.39.clone.1), dimensions={0}, to_apply=%region_16.21 | reduce | flops 8126464 | bytes 34603012 | tf_op jit(solution)/shard_map/reduce_sum | solution.py:121
  (113 shorter events, 53.4 us)
Async XLA Ops:
  7.2 57.0 %copy-start = (bf16[512,512]{1,0:T(8,128)(2,1)S(1)}, bf16[512,512]{1,0:T(8,128)(2,1)}, u32[]{:S(2)}) copy-start(bf16[512,512]{1,0:T(8,128)(2,1)} %param.18) | copy-start | bytes 1572868
  7.2 85.6 %copy-start.11 = (s32[2,16]{1,0:T(2,128)S(1)}, s32[2,16]{1,0:T(2,128)}, u32[]{:S(2)}) copy-start(s32[2,16]{1,0:T(2,128)} %param.22) | copy-start | bytes 388
  7.2 105.6 %copy-start.9 = (s32[2,512]{1,0:T(2,128)S(1)}, s32[2,512]{1,0:T(2,128)}, u32[]{:S(2)}) copy-start(s32[2,512]{1,0:T(2,128)} %param.19) | copy-start | bytes 12292
  9.3 21.7 %all-to-all-start = ((bf16[16,32,512]{2,1,0:T(8,128)(2,1)}), bf16[16,32,512]{2,1,0:T(8,128)(2,1)S(1)}, u32[]{:S(2)}, u32[]{:S(2)}) async-start(bf16[16,32,512]{2,1,0:T(8,128)(2,1)} %bitcast.6), calls=%async_computation | async-start | bytes 1048576 | tf_op jit(solution)/shard_map/all_to_all | solution.py:83
  18.3 115.0 %copy-start.10 = (f32[512]{0:T(512)S(1)}, f32[512]{0:T(512)}, u32[]{:S(2)}) copy-start(f32[512]{0:T(512)} %param.17) | copy-start | bytes 6148
  18.3 115.0 %copy-start.1 = (f32[512,512]{1,0:T(8,128)S(1)}, f32[512,512]{1,0:T(8,128)}, u32[]{:S(2)}) copy-start(f32[512,512]{1,0:T(8,128)} %param.16) | copy-start | bytes 3145732
  32.5 18.4 %all-to-all-start.1 = ((bf16[16,32,512]{2,1,0:T(8,128)(2,1)}), bf16[16,32,512]{2,1,0:T(8,128)(2,1)S(1)}, u32[]{:S(2)}, u32[]{:S(2)}) async-start(bf16[16,32,512]{2,1,0:T(8,128)(2,1)} %broadcast_select_fusion.2), calls=%async_computation.1 | async-start | bytes 1048576 | tf_op jit(solution)/shard_map/all_to_all | solution.py:86
  36.7 46.7 %reduce-scatter.3.cloned.1.call-start = ((), (), s32[]{:S(2)}) async-start(), calls=%async_computation.10 | async-start | bytes 786432 | tf_op jit(solution)/shard_map/reduce_scatter | solution.py:49
  64.2 6.1 %copy-start.2 = (bf16[512,512]{1,0:T(8,128)(2,1)}, bf16[512,512]{1,0:T(8,128)(2,1)S(1)}, u32[]{:S(2)}) copy-start(bf16[512,512]{1,0:T(8,128)(2,1)S(1)} %all_gather.12) | copy-start | bytes 1572868
  66.1 4.3 copy-start.4
  66.5 1.0 copy-start.7
  87.2 19.9 %all-to-all-start.2 = ((bf16[16,32,512]{2,1,0:T(8,128)(2,1)}), bf16[16,32,512]{2,1,0:T(8,128)(2,1)S(1)}, u32[]{:S(2)}, u32[]{:S(2)}) async-start(bf16[16,32,512]{2,1,0:T(8,128)(2,1)} %bitcast.74), calls=%async_computation.3 | async-start | bytes 1048576 | tf_op jit(solution)/shard_map/all_to_all | solution.py:92
  108.6 18.5 %all-to-all-start.3 = ((bf16[16,32,512]{2,1,0:T(8,128)(2,1)}), bf16[16,32,512]{2,1,0:T(8,128)(2,1)}, u32[]{:S(2)}, u32[]{:S(2)}) async-start(bf16[16,32,512]{2,1,0:T(8,128)(2,1)} %select_convert_fusion.1), calls=%async_computation.4 | async-start | bytes 1048576 | tf_op jit(solution)/shard_map/all_to_all | solution.py:99
  114.9 1.5 copy-start.5
  134.4 18.4 %all-to-all-start.4 = ((bf16[16,32,512]{2,1,0:T(8,128)(2,1)}), bf16[16,32,512]{2,1,0:T(8,128)(2,1)S(1)}, u32[]{:S(2)}, u32[]{:S(2)}) async-start(bf16[16,32,512]{2,1,0:T(8,128)(2,1)} %bitcast.21), calls=%async_computation.5 | async-start | bytes 1048576 | tf_op jit(solution)/shard_map/all_to_all | solution.py:83
  154.3 18.4 %all-to-all-start.5 = ((bf16[16,32,512]{2,1,0:T(8,128)(2,1)}), bf16[16,32,512]{2,1,0:T(8,128)(2,1)S(1)}, u32[]{:S(2)}, u32[]{:S(2)}) async-start(bf16[16,32,512]{2,1,0:T(8,128)(2,1)} %broadcast_select_fusion), calls=%async_computation.6 | async-start | bytes 1048576 | tf_op jit(solution)/shard_map/all_to_all | solution.py:86
  158.5 46.5 %reduce-scatter.5.cloned.1.call-start = ((), (), s32[]{:S(2)}) async-start(), calls=%async_computation.11 | async-start | bytes 786432 | tf_op jit(solution)/shard_map/reduce_scatter | solution.py:49
  187.8 0.8 copy-start.3
  188.3 1.0 copy-start.8
  190.6 223.0 %all-gather.3.cloned.1.call-start = ((), (), s32[]{:S(2)}) async-start(), calls=%async_computation.12 | async-start | bytes 34603008 | tf_op jit(solution)/shard_map/all_gather | solution.py:120
  194.4 0.8 copy-start.6
  208.7 25.3 %all-to-all-start.6 = ((bf16[16,32,512]{2,1,0:T(8,128)(2,1)}), bf16[16,32,512]{2,1,0:T(8,128)(2,1)S(1)}, u32[]{:S(2)}, u32[]{:S(2)}) async-start(bf16[16,32,512]{2,1,0:T(8,128)(2,1)} %bitcast.26), calls=%async_computation.8 | async-start | bytes 1048576 | tf_op jit(solution)/shard_map/all_to_all | solution.py:92
  235.5 25.6 %all-to-all-start.7 = ((bf16[16,32,512]{2,1,0:T(8,128)(2,1)}), bf16[16,32,512]{2,1,0:T(8,128)(2,1)S(1)}, u32[]{:S(2)}, u32[]{:S(2)}) async-start(bf16[16,32,512]{2,1,0:T(8,128)(2,1)} %select_convert_fusion), calls=%async_computation.9 | async-start | bytes 1048576 | tf_op jit(solution)/shard_map/all_to_all | solution.py:99
Sparse Core Ops, SparseCore 0:
  68.9 14.3 reduce-scatter.2
  190.7 13.4 reduce-scatter.4
  207.3 206.2 all-gather.2
